TPU v7x, 32 devices: a whole 2x2x4 slice. The times are simulated.
32 devices in a mesh: ctx: 8 (over y, x, core), wshard: 4 (over z).
Axes of the slice: x: 2, y: 2, z: 4, core: 2. Of those that a mesh axis runs over, the one named last changes fastest.
Arguments:
- byte_feats: bfloat16 [8, 2048, 768], P('wshard', 'ctx'), may hold values from -6 to 6
- lengths: int32 [8], P('wshard'), may hold values from 512 to 2048, as said below
- latent_array: bfloat16 [256, 1280], P('wshard'), may hold values from -6 to 6
- lat_gain: bfloat16 [1280], P('wshard'), may hold values from 0.5 to 1.5
- lat_bias: bfloat16 [1280], P('wshard'), may hold values from -4 to 4
- in_gain: bfloat16 [768], P('wshard'), may hold values from 0.5 to 1.5
- in_bias: bfloat16 [768], P('wshard'), may hold values from -4 to 4
- w_query: bfloat16 [1280, 256], P('wshard'), may hold values from -0.25 to 0.25
- w_key: bfloat16 [768, 256], P('wshard'), may hold values from -0.3125 to 0.3125
- w_value: bfloat16 [768, 1280], P('wshard'), may hold values from -0.21875 to 0.21875
- w_output: bfloat16 [1280, 1280], P('wshard'), may hold values from -2 to 2
- mlp_gain: bfloat16 [1280], P('wshard'), may hold values from 0.5 to 1.5
- mlp_bias: bfloat16 [1280], P('wshard'), may hold values from -4 to 4
- w_up: bfloat16 [1280, 1280], P('wshard'), may hold values from -0.15625 to 0.15625
- w_down: bfloat16 [1280, 1280], P('wshard'), may hold values from -0.15625 to 0.15625
- cotangent: bfloat16 [8, 256, 1280], P('wshard'), may hold values from -6 to 6
Outputs:
- latents_out: bfloat16 [8, 256, 1280], P('wshard')
- byte_grad: bfloat16 [8, 2048, 768], P('wshard', 'ctx')
- grad_latent: float32 [256, 1280], P('wshard')
- grad_lat_gain: float32 [1280], P('wshard')
- grad_lat_bias: float32 [1280], P('wshard')
- grad_in_gain: float32 [768], P('wshard')
- grad_in_bias: float32 [768], P('wshard')
- grad_query: float32 [1280, 256], P('wshard')
- grad_key: float32 [768, 256], P('wshard')
- grad_value: float32 [768, 1280], P('wshard')
- grad_output: float32 [1280, 1280], P('wshard')
- grad_mlp_gain: float32 [1280], P('wshard')
- grad_mlp_bias: float32 [1280], P('wshard')
- grad_up: float32 [1280, 1280], P('wshard')
- grad_down: float32 [1280, 1280], P('wshard')
Inputs may be any that keep to these rules, and one draw needn't show every extreme that they name: The first lengths[s] slots of sequence s hold bytes, the rest are padding; some sequence fills all 2048 slots.
All inputs are finite; a program needn't handle non-finite values.
Results may differ from a plain program's by a relative error of at most 0.019.
Values may be sent and summed in bfloat16 or wider, within the bound.
A program may use at most 256 MiB of HBM per device.

v0:
```python
import math
import jax
import jax.numpy as jnp
from jax import lax
from jax.sharding import PartitionSpec as P

H = 8
LOW = jnp.bfloat16
FULL = jnp.float32


def layer_norm(values, gain, offset):
    center = jnp.mean(values, axis=-1, keepdims=True)
    centred = values - center
    variance = jnp.mean(centred * centred, axis=-1, keepdims=True)
    return centred * lax.rsqrt(variance + 1e-05) * gain + offset


def exact_gelu(values):
    return jax.nn.gelu(values, approximate=False)


def matmul(left, right):
    return jnp.dot(left, right, preferred_element_type=FULL)


def matmul_tn(left, right):
    return lax.dot_general(left, right, (((0,), (0,)), ((), ())), preferred_element_type=FULL)


def matmul_nt(left, right):
    return lax.dot_general(left, right, (((1,), (1,)), ((), ())), preferred_element_type=FULL)


def gather(shard):
    return lax.all_gather(shard, "wshard", axis=0, tiled=True)


def scatter(total):
    return lax.psum_scatter(total.astype(LOW), "wshard", scatter_dimension=0, tiled=True).astype(
        FULL
    )


def own_part(total, shard):
    size = shard.shape[0]
    return lax.dynamic_slice_in_dim(total, lax.axis_index("wshard") * size, size, 0)


def shards(
    byte_feats,
    lengths,
    latent_array,
    lat_gain,
    lat_bias,
    in_gain,
    in_bias,
    w_query,
    w_key,
    w_value,
    w_output,
    mlp_gain,
    mlp_bias,
    w_up,
    w_down,
    cotangent,
):
    seqs, slots, width = byte_feats.shape
    gain_in, bias_in = (gather(in_gain).astype(FULL), gather(in_bias).astype(FULL))
    key_w, value_w = (gather(w_key), gather(w_value))
    latent = gather(latent_array).astype(FULL)
    gain_lat, bias_lat = (gather(lat_gain).astype(FULL), gather(lat_bias).astype(FULL))
    query_w = gather(w_query)
    gain_mlp, bias_mlp = (gather(mlp_gain).astype(FULL), gather(mlp_bias).astype(FULL))
    output_w, up_w, down_w = (gather(w_output), gather(w_up), gather(w_down))
    features = byte_feats.reshape(seqs * slots, width).astype(FULL)
    normed_in, in_back = jax.vjp(layer_norm, features, gain_in, bias_in)
    input_low = normed_in.astype(LOW)
    keys = matmul(input_low, key_w).astype(LOW)
    values = matmul(input_low, value_w).astype(LOW)
    normed_lat, lat_back = jax.vjp(layer_norm, latent, gain_lat, bias_lat)
    lat_low = normed_lat.astype(LOW)
    rows = lat_low.shape[0]
    queries = matmul(lat_low, query_w).astype(LOW)
    score_scale = 1.0 / math.sqrt(queries.shape[1] // H)
    qheads = queries.reshape(rows, H, -1)
    kheads = keys.reshape(seqs, slots, H, -1)
    vheads = values.reshape(seqs, slots, H, -1)
    scores = jnp.einsum("lhd,mkhd->mhlk", qheads, kheads, preferred_element_type=FULL) * score_scale
    slot_ids = lax.axis_index("ctx") * slots + lax.iota(jnp.int32, slots)
    valid = (slot_ids[None, :] < lengths[:, None])[:, None, None, :]
    scores = jnp.where(valid, scores, -1e30)
    highest = lax.pmax(jnp.max(scores, axis=-1), "ctx")
    weights = jnp.where(valid, jnp.exp(scores - highest[..., None]), 0.0)
    total = lax.psum(jnp.sum(weights, axis=-1), "ctx")
    numer = jnp.einsum("mhlk,mkhe->mlhe", weights.astype(LOW), vheads, preferred_element_type=FULL)
    numer = lax.psum(numer.astype(LOW), "ctx").astype(FULL)
    attended = numer / jnp.transpose(total, (0, 2, 1))[..., None]
    attended = attended.reshape(seqs * rows, -1)
    att_low = attended.astype(LOW)
    hidden = jnp.tile(latent, (seqs, 1)) + matmul(att_low, output_w)
    normed_mid, mid_back = jax.vjp(layer_norm, hidden, gain_mlp, bias_mlp)
    mid_low = normed_mid.astype(LOW)
    upward = matmul(mid_low, up_w)
    activated, gelu_back = jax.vjp(exact_gelu, upward)
    act_low = activated.astype(LOW)
    result = hidden + matmul(act_low, down_w)
    dout_low = cotangent.reshape(seqs * rows, -1)
    grad_down = scatter(matmul_tn(act_low, dout_low))
    (grad_upward,) = gelu_back(matmul_nt(dout_low, down_w))
    up_low = grad_upward.astype(LOW)
    grad_up = scatter(matmul_tn(mid_low, up_low))
    dhid_norm, grad_gmlp, grad_bmlp = mid_back(matmul_nt(up_low, up_w))
    dhidden = dout_low.astype(FULL) + dhid_norm
    dhid_low = dhidden.astype(LOW)
    grad_output = scatter(matmul_tn(att_low, dhid_low))
    grad_hidden = scatter(jnp.sum(dhidden.reshape(seqs, rows, -1), axis=0))
    grad_att = matmul_nt(dhid_low, output_w).astype(LOW)
    grad_heads = grad_att.reshape(seqs, rows, H, -1)
    delta = jnp.sum(
        grad_heads.astype(FULL) * attended.reshape(seqs, rows, H, -1), axis=-1
    ).transpose(0, 2, 1)
    probs = weights / total[..., None]
    dprobs = jnp.einsum("mlhe,mkhe->mhlk", grad_heads, vheads, preferred_element_type=FULL)
    dscores = (probs * (dprobs - delta[..., None])).astype(LOW)
    dquery = (
        jnp.einsum("mhlk,mkhd->lhd", dscores, kheads, preferred_element_type=FULL) * score_scale
    )
    dkeys = jnp.einsum("mhlk,lhd->mkhd", dscores, qheads, preferred_element_type=FULL) * score_scale
    dvalues = jnp.einsum(
        "mhlk,mlhe->mkhe", probs.astype(LOW), grad_heads, preferred_element_type=FULL
    )
    dkeys = dkeys.astype(LOW).reshape(seqs * slots, -1)
    dvalues = dvalues.astype(LOW).reshape(seqs * slots, -1)
    dquery = lax.psum(dquery.reshape(rows, -1).astype(LOW), ("ctx", "wshard"))
    grad_query = matmul_tn(
        lax.dynamic_slice_in_dim(
            lat_low, lax.axis_index("wshard") * w_query.shape[0], w_query.shape[0], 1
        ),
        dquery,
    )
    dlat_norm, grad_glat, grad_blat = lat_back(matmul_nt(dquery, query_w))
    grad_latent = grad_hidden + own_part(dlat_norm, latent_array)
    dnorm_in = matmul_nt(dkeys, key_w) + matmul_nt(dvalues, value_w)
    dfeatures, grad_gin, grad_bin = in_back(dnorm_in)
    grad_key = lax.psum(scatter(matmul_tn(input_low, dkeys)).astype(LOW), "ctx").astype(FULL)
    grad_value = lax.psum(scatter(matmul_tn(input_low, dvalues)).astype(LOW), "ctx").astype(FULL)
    in_sums = lax.psum(jnp.concatenate([grad_gin, grad_bin]), ("ctx", "wshard"))
    grad_gin, grad_bin = jnp.split(in_sums, 2)
    mlp_sums = lax.psum(jnp.concatenate([grad_gmlp, grad_bmlp]), "wshard")
    grad_gmlp, grad_bmlp = jnp.split(mlp_sums, 2)
    return (
        result.astype(LOW).reshape(seqs, rows, -1),
        dfeatures.astype(LOW).reshape(seqs, slots, width),
        grad_latent,
        own_part(grad_glat, lat_gain),
        own_part(grad_blat, lat_bias),
        own_part(grad_gin, in_gain),
        own_part(grad_bin, in_bias),
        grad_query,
        grad_key,
        grad_value,
        grad_output,
        own_part(grad_gmlp, mlp_gain),
        own_part(grad_bmlp, mlp_bias),
        grad_up,
        grad_down,
    )


def solution(mesh):
    sharded, plain = (P("wshard", None), P("wshard"))
    return jax.shard_map(
        shards,
        mesh=mesh,
        in_specs=(
            P("wshard", "ctx", None),
            plain,
            sharded,
            plain,
            plain,
            plain,
            plain,
            sharded,
            sharded,
            sharded,
            sharded,
            plain,
            plain,
            sharded,
            sharded,
            P("wshard", None, None),
        ),
        out_specs=(
            P("wshard", None, None),
            P("wshard", "ctx", None),
            sharded,
            plain,
            plain,
            plain,
            plain,
            sharded,
            sharded,
            sharded,
            sharded,
            plain,
            plain,
            sharded,
            sharded,
        ),
        check_vma=False,
    )
```

profile of v0, /device:TPU:0, one launch (start us, length us, event | category | flops | bytes accessed | tf_op | source)
XLA Modules:
  0.0 920.5 jit_solution(9357087982869084946)
XLA Ops:
  8.1 22.5 %all_gather.39 = bf16[256,1280]{1,0:T(8,128)(2,1)S(1)} all-gather(bf16[64,1280]{1,0:T(8,128)(2,1)} %param.18), channel_id=1, replica_groups=mesh['ctx'=8,'wshard'=4] {'wshard'}, dimensions={0}, use_global_device_ids=true | all-gather | bytes 819200 | tf_op jit(solution)/shard_map/all_gather | solution.py:36
  35.1 19.8 %all-reduce.7 = (bf16[1280]{0:T(1024)(128)(2,1)S(1)}, bf16[1280]{0:T(1024)(128)(2,1)S(1)}, bf16[768]{0:T(1024)(128)(2,1)S(1)}, bf16[768]{0:T(1024)(128)(2,1)S(1)...) all-reduce(bf16[1280]{0:T(1024)(128)(2,1)S(1)} %dynamic-update-slic, ...), channel_id=1, replica_groups=mesh['ctx'=8,'wshard'=4] {'wshard'}, use_global_device_ids=true, to_apply=%add.3 | all-reduce | flops 6656 | bytes 26624
  56.1 15.5 %all_gather.43 = bf16[768,256]{1,0:T(8,128)(2,1)S(1)} all-gather(bf16[192,256]{1,0:T(8,128)(2,1)S(1)} %copy-done.36), channel_id=1, replica_groups=mesh['ctx'=8,'wshard'=4] {'wshard'}, dimensions={0}, use_global_device_ids=true | all-gather | bytes 491520 | tf_op jit(solution)/shard_map/all_gather | solution.py:36
  73.1 15.1 %all_gather.46 = bf16[1280,256]{1,0:T(8,128)(2,1)S(1)} all-gather(bf16[320,256]{1,0:T(8,128)(2,1)S(1)} %copy-done.30), channel_id=1, replica_groups=mesh['ctx'=8,'wshard'=4] {'wshard'}, dimensions={0}, use_global_device_ids=true | all-gather | bytes 819200 | tf_op jit(solution)/shard_map/all_gather | solution.py:36
  93.5 22.3 %pmax.7 = f32[2,8,256]{2,0,1:T(2,128)S(1)} all-reduce(f32[2,8,256]{2,0,1:T(2,128)S(1)} %get-tuple-element.50), channel_id=1, replica_groups=mesh['ctx'=8,'wshard'=4] {'ctx'}, use_global_device_ids=true, to_apply=%region_5.6 | all-reduce | flops 4096 | bytes 32768 | tf_op jit(solution)/shard_map/pmax | solution.py:93
  115.8 3.4 fusion.37
  119.2 22.3 %psum.50 = f32[2,8,256]{2,0,1:T(2,128)S(1)} all-reduce(f32[2,8,256]{2,0,1:T(2,128)S(1)} %fusion.37), channel_id=1, replica_groups=mesh['ctx'=8,'wshard'=4] {'ctx'}, use_global_device_ids=true, to_apply=%region_8.9 | all-reduce | flops 4096 | bytes 32768 | tf_op jit(solution)/shard_map/psum | solution.py:95
  141.6 4.4 fusion.14
  146.0 3.8 convolution_convert_fusion.4
  152.6 3.6 fusion.24
  159.7 53.1 %all-reduce.12.cloned.1.call-done = bf16[2,256,8,160]{1,3,2,0:T(8,128)(2,1)} async-done(((bf16[2,256,8,160]{1,3,2,0:T(8,128)(2,1)}), bf16[2,256,8,160]{1,3,2,0:T(8,128)(2,1)}) %all-reduce.12.cloned.1.call-update) | async-done | bytes 1310736 | tf_op jit(solution)/shard_map/psum | solution.py:97
  216.0 63.3 %all-gather.7.cloned.1.call-done = bf16[1280,1280]{1,0:T(8,128)(2,1)} async-done(((bf16[320,1280]{1,0:T(8,128)(2,1)}), bf16[1280,1280]{1,0:T(8,128)(2,1)}) %all-gather.7.cloned.1.call-update) | async-done | bytes 3276816 | tf_op jit(solution)/shard_map/all_gather | solution.py:36
  285.2 60.0 %all-gather.9.cloned.1.call-done = bf16[1280,1280]{1,0:T(8,128)(2,1)} async-done(((bf16[320,1280]{1,0:T(8,128)(2,1)}), bf16[1280,1280]{1,0:T(8,128)(2,1)}) %all-gather.9.cloned.1.call-update) | async-done | bytes 3276816 | tf_op jit(solution)/shard_map/all_gather | solution.py:36
  345.1 6.2 fusion.51
  351.4 59.6 %all-gather.11.cloned.1.call-done = bf16[1280,1280]{1,0:T(8,128)(2,1)} async-done(((bf16[320,1280]{1,0:T(8,128)(2,1)}), bf16[1280,1280]{1,0:T(8,128)(2,1)}) %all-gather.11.cloned.1.call-update) | async-done | bytes 3276816 | tf_op jit(solution)/shard_map/all_gather | solution.py:36
  410.9 11.0 %add_convert_fusion = (bf16[512,1280]{1,0:T(8,128)(2,1)S(1)}, f32[512,1280]{1,0:T(8,128)}) fusion(f32[512,1280]{1,0:T(8,128)} %fusion.51, bf16[512,1280]{1,0:T(8,128)(2,1)S(1)} %bitcast.132, bf16[1280,1280]{1,0:T(8,128)(2,1)} %all-gather.11.cloned.1.call-done), kind=kOutput, calls=%fused_computation.22 | convolution fusion | flops 1724907520 | bytes 11141120 | tf_op jit(solution)/shard_map/dot_general | solution.py:32
  433.9 4.0 reshape.264
  440.0 4.2 multiply_convert_fusion
  460.7 5.9 reduce-scatter.9.cloned.1.call-done
  466.6 42.1 %reduce-scatter.11.cloned.1.call-done = bf16[192,1280]{1,0:T(8,128)(2,1)} async-done(((bf16[768,1280]{1,0:T(8,128)(2,1)}), bf16[192,1280]{1,0:T(8,128)(2,1)}) %reduce-scatter.11.cloned.1.call-update) | async-done | bytes 491536 | tf_op jit(solution)/shard_map/reduce_scatter | solution.py:40
  508.7 5.3 convolution_convert_fusion.2
  515.4 5.7 convolution_convert_fusion.1
  525.3 3.7 convolution_convert_fusion
  534.3 39.6 %psum.52 = f32[1536]{0:T(1024)S(1)} all-reduce(f32[1536]{0:T(1024)S(1)} %pad_maximum_fusion.1), channel_id=1, replica_groups=mesh['ctx'=8,'wshard'=4] {'ctx','wshard'}, use_global_device_ids=true, to_apply=%region_25.26 | all-reduce | flops 1536 | bytes 12288 | tf_op jit(solution)/shard_map/psum | solution.py:148
  575.1 17.7 %psum.55 = f32[2560]{0:T(1024)S(1)} all-reduce(f32[2560]{0:T(1024)S(1)} %pad_maximum_fusion), channel_id=1, replica_groups=mesh['ctx'=8,'wshard'=4] {'wshard'}, use_global_device_ids=true, to_apply=%region_33.34 | all-reduce | flops 2560 | bytes 20480 | tf_op jit(solution)/shard_map/psum | solution.py:150
  596.5 5.0 fusion.2
  601.5 35.1 %all-reduce.14.cloned.1.call-done = bf16[256,256]{0,1:T(8,128)(2,1)} async-done(((bf16[256,256]{0,1:T(8,128)(2,1)}), bf16[256,256]{0,1:T(8,128)(2,1)}) %all-reduce.14.cloned.1.call-update) | async-done | bytes 131088 | tf_op jit(solution)/shard_map/psum | solution.py:135
  642.3 18.4 %reduce-scatter.7.cloned.1.call-done = bf16[64,1280]{1,0:T(8,128)(2,1)} async-done(((bf16[256,1280]{1,0:T(8,128)(2,1)}), bf16[64,1280]{1,0:T(8,128)(2,1)}) %reduce-scatter.7.cloned.1.call-update) | async-done | bytes 163856 | tf_op jit(solution)/shard_map/reduce_scatter | solution.py:40
  662.5 55.3 %all-reduce.16.cloned.1.call-done = (bf16[192,256]{1,0:T(8,128)(2,1)}, bf16[192,1280]{1,0:T(8,128)(2,1)}) async-done(((bf16[192,256]{1,0:T(8,128)(2,1)}, bf16[192,1280]{1,0:T(8,128)(2,1)}), (bf16[192,256]{1,0:T(8,128)(2,1)}, bf16[192,1280]{1,0:T(8,128)(2,1)})) %all-reduce.16.cloned.1.call-update) | async-done | bytes 589840 | tf_op jit(solution)/shard_map/psum | solution.py:146
  721.4 60.4 %reduce-scatter.13.cloned.1.call-done = bf16[320,1280]{1,0:T(8,128)(2,1)} async-done(((bf16[1280,1280]{1,0:T(8,128)(2,1)}), bf16[320,1280]{1,0:T(8,128)(2,1)}) %reduce-scatter.13.cloned.1.call-update) | async-done | bytes 819216 | tf_op jit(solution)/shard_map/reduce_scatter | solution.py:40
  784.2 62.3 %reduce-scatter.15.cloned.1.call-done = bf16[320,1280]{1,0:T(8,128)(2,1)} async-done(((bf16[1280,1280]{1,0:T(8,128)(2,1)}), bf16[320,1280]{1,0:T(8,128)(2,1)}) %reduce-scatter.15.cloned.1.call-update) | async-done | bytes 819216 | tf_op jit(solution)/shard_map/reduce_scatter | solution.py:40
  848.9 62.4 %reduce-scatter.17.cloned.1.call-done = bf16[320,1280]{1,0:T(8,128)(2,1)} async-done(((bf16[1280,1280]{1,0:T(8,128)(2,1)}), bf16[320,1280]{1,0:T(8,128)(2,1)}) %reduce-scatter.17.cloned.1.call-update) | async-done | bytes 819216 | tf_op jit(solution)/shard_map/reduce_scatter | solution.py:40
  (272 shorter events, 91.3 us)
Async XLA Ops:
  7.2 47.6 %copy-start = (bf16[2,256,768]{2,1,0:T(8,128)(2,1)S(1)}, bf16[2,256,768]{2,1,0:T(8,128)(2,1)}, u32[]{:S(2)}) copy-start(bf16[2,256,768]{2,1,0:T(8,128)(2,1)} %param.16) | copy-start | bytes 2359300
  7.3 48.8 %copy-start.36 = (bf16[192,256]{1,0:T(8,128)(2,1)S(1)}, bf16[192,256]{1,0:T(8,128)(2,1)}, u32[]{:S(2)}) copy-start(bf16[192,256]{1,0:T(8,128)(2,1)} %param.24) | copy-start | bytes 294916
  7.3 138.7 %all-gather.5.cloned.1.call-start = ((), (), s32[]{:S(2)}) async-start(), calls=%async_computation.6 | async-start | bytes 2457600 | tf_op jit(solution)/shard_map/all_gather | solution.py:36
  8.0 204.7 %all-reduce.12.cloned.1.call-start = ((), (), s32[]{:S(2)}) async-start(), calls=%async_computation.7 | async-start | bytes 2621440 | tf_op jit(solution)/shard_map/psum | solution.py:97
  33.3 55.0 %copy-start.51 = (f32[256]{0:T(256)}, f32[256]{0:T(256)S(1)}, u32[]{:S(2)}) copy-start(f32[256]{0:T(256)S(1)} %broadcast_multiply_fusion.2) | copy-start | bytes 3076
  54.9 103.5 %copy-start.34 = (f32[768]{0:T(1024)}, f32[768]{0:T(1024)S(1)}, u32[]{:S(2)}) copy-start(f32[768]{0:T(1024)S(1)} %convert_element_type.170) | copy-start | bytes 9220
  73.1 68.5 %copy-start.39 = (pred[2,256]{1,0:T(4,128)(4,1)}, pred[2,256]{1,0:T(4,128)(4,1)S(1)}, u32[]{:S(2)}) copy-start(pred[2,256]{1,0:T(4,128)(4,1)S(1)} %broadcast_compare_fusion) | copy-start | bytes 1540
  156.2 123.1 %all-gather.7.cloned.1.call-start = ((), (), s32[]{:S(2)}) async-start(), calls=%async_computation.8 | async-start | bytes 4096000 | tf_op jit(solution)/shard_map/all_gather | solution.py:36
  157.0 188.1 %all-gather.9.cloned.1.call-start = ((), (), s32[]{:S(2)}) async-start(), calls=%async_computation.9 | async-start | bytes 4096000 | tf_op jit(solution)/shard_map/all_gather | solution.py:36
  157.6 253.4 %all-gather.11.cloned.1.call-start = ((), (), s32[]{:S(2)}) async-start(), calls=%async_computation.10 | async-start | bytes 4096000 | tf_op jit(solution)/shard_map/all_gather | solution.py:36
  158.1 308.5 %reduce-scatter.9.cloned.1.call-start = ((), (), s32[]{:S(2)}) async-start(), calls=%async_computation.13 | async-start | bytes 491520 | tf_op jit(solution)/shard_map/reduce_scatter | solution.py:40
  158.4 186.7 %copy-start.59 = (f32[1280]{0:T(1024)}, f32[1280]{0:T(1024)S(1)}, u32[]{:S(2)}) copy-start(f32[1280]{0:T(1024)S(1)} %convert_element_type.186) | copy-start | bytes 15364
  158.4 266.3 %copy-start.45 = (f32[1280]{0:T(1024)}, f32[1280]{0:T(1024)S(1)}, u32[]{:S(2)}) copy-start(f32[1280]{0:T(1024)S(1)} %convert_element_type.185) | copy-start | bytes 15364
  216.0 67.3 %copy-start.7 = (bf16[160,8,2,256]{3,1,2,0:T(8,128)(2,1)}, bf16[160,8,2,256]{3,1,2,0:T(8,128)(2,1)S(1)}, u32[]{:S(2)}) copy-start(bf16[160,8,2,256]{3,1,2,0:T(8,128)(2,1)S(1)} %copy.95) | copy-start | bytes 3932164
  283.3 141.4 %copy-start.49 = (f32[512]{0:T(512)}, f32[512]{0:T(512)S(1)}, u32[]{:S(2)}) copy-start(f32[512]{0:T(512)S(1)} %broadcast_multiply_fusion) | copy-start | bytes 6148
  285.1 139.6 %copy-start.61 = (f32[512]{0:T(512)}, f32[512]{0:T(512)S(1)}, u32[]{:S(2)}) copy-start(f32[512]{0:T(512)S(1)} %fusion.45) | copy-start | bytes 6148
  285.2 125.8 %copy-start.24 = (bf16[2,256,1280]{2,1,0:T(8,128)(2,1)S(1)}, bf16[2,256,1280]{2,1,0:T(8,128)(2,1)}, u32[]{:S(2)}) copy-start(bf16[2,256,1280]{2,1,0:T(8,128)(2,1)} %param.31) | copy-start | bytes 3932164
  447.2 61.5 %reduce-scatter.11.cloned.1.call-start = ((), (), s32[]{:S(2)}) async-start(), calls=%async_computation.14 | async-start | bytes 2457600 | tf_op jit(solution)/shard_map/reduce_scatter | solution.py:40
  455.4 181.2 %all-reduce.14.cloned.1.call-start = ((), (), s32[]{:S(2)}) async-start(), calls=%async_computation.12 | async-start | bytes 262144 | tf_op jit(solution)/shard_map/psum | solution.py:135
  457.5 51.3 %copy-start.8 = (bf16[160,8,2,256]{3,1,2,0:T(8,128)(2,1)S(1)}, bf16[160,8,2,256]{3,1,2,0:T(8,128)(2,1)}, u32[]{:S(2)}) copy-start(bf16[160,8,2,256]{3,1,2,0:T(8,128)(2,1)} %copy-done.7) | copy-start | bytes 3932164
  457.5 203.2 %reduce-scatter.7.cloned.1.call-start = ((), (), s32[]{:S(2)}) async-start(), calls=%async_computation.11 | async-start | bytes 819200 | tf_op jit(solution)/shard_map/reduce_scatter | solution.py:40
  460.6 257.1 %all-reduce.16.cloned.1.call-start = ((), (), s32[]{:S(2)}) async-start(), calls=%async_computation.18 | async-start | bytes 1179648 | tf_op jit(solution)/shard_map/psum | solution.py:146
  508.7 273.1 %reduce-scatter.13.cloned.1.call-start = ((), (), s32[]{:S(2)}) async-start(), calls=%async_computation.15 | async-start | bytes 4096000 | tf_op jit(solution)/shard_map/reduce_scatter | solution.py:40
  514.1 332.4 %reduce-scatter.15.cloned.1.call-start = ((), (), s32[]{:S(2)}) async-start(), calls=%async_computation.16 | async-start | bytes 4096000 | tf_op jit(solution)/shard_map/reduce_scatter | solution.py:40
  521.1 390.3 %reduce-scatter.17.cloned.1.call-start = ((), (), s32[]{:S(2)}) async-start(), calls=%async_computation.17 | async-start | bytes 4096000 | tf_op jit(solution)/shard_map/reduce_scatter | solution.py:40
  533.3 41.8 %copy-start.57 = (f32[1280]{0:T(1024)S(1)}, f32[1280]{0:T(1024)}, u32[]{:S(2)}) copy-start(f32[1280]{0:T(1024)} %get-tuple-element.15) | copy-start | bytes 15364
  533.3 41.8 %copy-start.58 = (f32[1280]{0:T(1024)S(1)}, f32[1280]{0:T(1024)}, u32[]{:S(2)}) copy-start(f32[1280]{0:T(1024)} %get-tuple-element.17) | copy-start | bytes 15364
  533.3 60.8 %copy-start.48 = (f32[1,2,2,128]{3,1,2,0:T(2,128)S(1)}, f32[1,2,2,128]{3,1,2,0:T(2,128)}, u32[]{:S(2)}) copy-start(f32[1,2,2,128]{3,1,2,0:T(2,128)} %copy-done.47) | copy-start | bytes 6148
  596.5 40.1 %copy-start.17 = (bf16[1280,256]{1,0:T(8,128)(2,1)S(1)}, bf16[1280,256]{1,0:T(8,128)(2,1)}, u32[]{:S(2)}) copy-start(bf16[1280,256]{1,0:T(8,128)(2,1)} %copy-done.16) | copy-start | bytes 1966084
  596.5 40.1 %copy-start.38 = (f32[1280]{0:T(1024)S(1)}, f32[1280]{0:T(1024)}, u32[]{:S(2)}) copy-start(f32[1280]{0:T(1024)} %copy-done.37) | copy-start | bytes 15364
  596.5 40.1 %copy-start.52 = (f32[256]{0:T(256)S(1)}, f32[256]{0:T(256)}, u32[]{:S(2)}) copy-start(f32[256]{0:T(256)} %copy-done.51) | copy-start | bytes 3076
  596.5 40.1 %copy-start.54 = (f32[256]{0:T(256)S(1)}, f32[256]{0:T(256)}, u32[]{:S(2)}) copy-start(f32[256]{0:T(256)} %copy-done.53) | copy-start | bytes 3076
  (54 other events, 482.7 us)
Sparse Core Ops, SparseCore 0:
  9.7 52.2 all-gather.4
  156.4 56.3 all-reduce.11
  214.4 64.8 all-gather.6
  280.8 64.2 all-gather.8
  346.6 64.2 all-gather.10
  447.3 19.2 reduce-scatter.8
  468.9 39.7 reduce-scatter.10
  514.8 121.7 all-reduce.13
  639.5 21.1 reduce-scatter.6
  663.7 53.9 all-reduce.15
  720.2 61.5 reduce-scatter.12
  784.0 62.4 reduce-scatter.14
  848.9 62.3 reduce-scatter.16
where the time goes:
time: 929 us; the launch traced here: 920 us
  waiting for transfers between devices  580 us (62%)
  blocking collectives  175 us (19%)
  matrix products  76.7 us (8%)
  other arithmetic  36.8 us (4%)
  local copies, waits for them, and re-layouts  34.6 us (4%)
  between operations  16.3 us (2%)
    reduce_scatter x6, waiting for transfers between devices, scatter(): lax.psum_scatter(total.astype(LOW), 'wshard', scatter_dimension=0, tiled=...  252 us
    all_gather x4, waiting for transfers between devices, gather(): return lax.all_gather(shard, 'wshard', axis=0, tiled=True)  183 us
    psum x1, waiting for transfers between devices, shards(): lax.psum(scatter(matmul_tn(input_low, dkeys)).astype(LOW), 'ctx')  55.3 us
    psum x1, waiting for transfers between devices, shards(): numer = lax.psum(numer.astype(LOW), 'ctx').astype(FULL)  53.1 us
    all_gather x3, blocking collectives, gather(): return lax.all_gather(shard, 'wshard', axis=0, tiled=True)  53 us
    psum x1, blocking collectives, shards(): in_sums = lax.psum(jnp.concatenate([grad_gin, grad_bin]), ('ctx', 'wshard'))  39.6 us
    psum x1, waiting for transfers between devices, shards(): dquery = lax.psum(dquery.reshape(rows, -1).astype(LOW), ('ctx', 'wshard'))  35.1 us
    psum x1, blocking collectives, shards(): total = lax.psum(jnp.sum(weights, axis=-1), 'ctx')  22.3 us
  transfers between devices with their start and end apart: 13, of which 12 were waited for; matrix products, arithmetic and copies ran while one was open for 10% of the time, Pallas kernels for 0%

commit v1 on v0

--- a/solution.py
+++ b/solution.py
@@ -9,6 +9,18 @@
 FULL = jnp.float32
 
 
+def doubled_up(x, axis, dim):
+    ways, here = (lax.axis_size(axis), lax.axis_index(axis))
+    grown, reach = (x, 1)
+    while reach < ways:
+        theirs = lax.ppermute(grown, axis, [(d, d ^ reach) for d in range(ways)])
+        mine_first = jnp.concatenate([grown, theirs], axis=dim)
+        theirs_first = jnp.concatenate([theirs, grown], axis=dim)
+        grown = jnp.where(here & reach == 0, mine_first, theirs_first)
+        reach = 2 * reach
+    return grown
+
+
 def layer_norm(values, gain, offset):
     center = jnp.mean(values, axis=-1, keepdims=True)
     centred = values - center
@@ -33,7 +45,7 @@
 
 
 def gather(shard):
-    return lax.all_gather(shard, "wshard", axis=0, tiled=True)
+    return doubled_up(shard, "wshard", 0)
 
 
 def scatter(total):

time: 929 us -> 931 us (level)
  blocking collectives: 175 us -> 102 us
  starting transfers between devices: 0.87 us -> 44.7 us
  other arithmetic: 36.8 us -> 56.4 us
  matrix products: 76.7 us -> 89.1 us
  waiting for transfers between devices: 580 us -> 591 us
    ppermute x0 -> x26, waiting for transfers between devices: none -> 199 us  [doubled_up(): theirs = lax.ppermute(grown, axis, [(d, d ^ reach) for d in range(ways)])]
    all_gather x4 -> x0, waiting for transfers between devices: 183 us -> none  [gather(): return lax.all_gather(shard, 'wshard', axis=0, tiled=True)]
    all_gather x3 -> x0, blocking collectives: 53 us -> none  [gather(): return lax.all_gather(shard, 'wshard', axis=0, tiled=True)]
    ppermute x0 -> x26, starting transfers between devices: none -> 43.9 us  [doubled_up(): theirs = lax.ppermute(grown, axis, [(d, d ^ reach) for d in range(ways)])]
    unnamed x1 -> x0, blocking collectives: 19.8 us -> none
    select_n x0 -> x13, other arithmetic: none -> 18.1 us  [doubled_up(): grown = jnp.where(here & reach == 0, mine_first, theirs_first)]
  transfers between devices with their start and end apart: 13 -> 35, of which waited for: 12 -> 24; matrix products, arithmetic and copies ran while one was open for 10% -> 14% of each run, Pallas kernels for 0% -> 0%
where the time goes in v1:
time: 931 us; the launch traced here: 923 us
  waiting for transfers between devices  591 us (63%)
  blocking collectives  102 us (11%)
  matrix products  89.1 us (10%)
  other arithmetic  56.4 us (6%)
  starting transfers between devices  44.7 us (5%)
  local copies, waits for them, and re-layouts  25.4 us (3%)
  between operations  15 us (2%)
    reduce_scatter x6, waiting for transfers between devices, scatter(): lax.psum_scatter(total.astype(LOW), 'wshard', scatter_dimension=0, tiled=...  252 us
    ppermute x26, waiting for transfers between devices, doubled_up(): theirs = lax.ppermute(grown, axis, [(d, d ^ reach) for d in range(ways)])  199 us
    psum x1, waiting for transfers between devices, shards(): lax.psum(scatter(matmul_tn(input_low, dkeys)).astype(LOW), 'ctx')  55.3 us
    psum x1, waiting for transfers between devices, shards(): numer = lax.psum(numer.astype(LOW), 'ctx').astype(FULL)  46.5 us
    ppermute x26, starting transfers between devices, doubled_up(): theirs = lax.ppermute(grown, axis, [(d, d ^ reach) for d in range(ways)])  43.9 us
    psum x1, blocking collectives, shards(): in_sums = lax.psum(jnp.concatenate([grad_gin, grad_bin]), ('ctx', 'wshard'))  37.8 us
    psum x1, waiting for transfers between devices, shards(): dquery = lax.psum(dquery.reshape(rows, -1).astype(LOW), ('ctx', 'wshard'))  37.5 us
    dot_general x6, matrix products, matmul(): return jnp.dot(left, right, preferred_element_type=FULL)  27 us
  transfers between devices with their start and end apart: 35, of which 24 were waited for; matrix products, arithmetic and copies ran while one was open for 14% of the time, Pallas kernels for 0%

profile of v1, /device:TPU:0, one launch (start us, length us, event | category | flops | bytes accessed | tf_op | source)
XLA Modules:
  0.0 923.1 jit_solution(3374845455109183755)
XLA Ops:
  28.4 8.3 collective-permute-done.18
  75.0 34.4 %collective-permute-done.9 = bf16[384,256]{1,0:T(8,128)(2,1)S(1)} collective-permute-done((bf16[384,256]{1,0:T(8,128)(2,1)S(1)}, bf16[384,256]{1,0:T(8,128)(2,1)S(1)}, u32[]{:S(2)}, u32[]{:S(2)}) %collective-permute-start.9) | collective-permute-done | bytes 196640 | tf_op jit(solution)/shard_map/ppermute | solution.py:16
  120.8 9.4 %collective-permute-done.15 = bf16[640,256]{1,0:T(8,128)(2,1)S(1)} collective-permute-done((bf16[640,256]{1,0:T(8,128)(2,1)S(1)}, bf16[640,256]{1,0:T(8,128)(2,1)S(1)}, u32[]{:S(2)}, u32[]{:S(2)}) %collective-permute-start.15) | collective-permute-done | bytes 327712 | tf_op jit(solution)/shard_map/ppermute | solution.py:16
  133.7 22.3 %pmax.7 = f32[2,8,256]{2,0,1:T(2,128)S(1)} all-reduce(f32[2,8,256]{2,0,1:T(2,128)S(1)} %get-tuple-element.44), channel_id=1, replica_groups=mesh['ctx'=8,'wshard'=4] {'ctx'}, use_global_device_ids=true, to_apply=%region_5.6 | all-reduce | flops 4096 | bytes 32768 | tf_op jit(solution)/shard_map/pmax | solution.py:105
  164.7 24.1 %psum.50 = f32[2,8,256]{2,0,1:T(2,128)S(1)} all-reduce(f32[2,8,256]{2,0,1:T(2,128)S(1)} %fusion.39), channel_id=1, replica_groups=mesh['ctx'=8,'wshard'=4] {'ctx'}, use_global_device_ids=true, to_apply=%region_8.9 | all-reduce | flops 4096 | bytes 32768 | tf_op jit(solution)/shard_map/psum | solution.py:107
  188.8 4.4 fusion.14
  196.3 42.2 %collective-permute-done.7 = bf16[384,1280]{1,0:T(8,128)(2,1)} collective-permute-done((bf16[384,1280]{1,0:T(8,128)(2,1)S(1)}, bf16[384,1280]{1,0:T(8,128)(2,1)}, u32[]{:S(2)}, u32[]{:S(2)}) %collective-permute-start.7) | collective-permute-done | bytes 983072 | tf_op jit(solution)/shard_map/ppermute | solution.py:16
  238.5 3.8 convolution_convert_fusion.4
  258.9 46.5 %all-reduce.5.cloned.1.call-done = bf16[2,256,8,160]{1,3,2,0:T(8,128)(2,1)} async-done(((bf16[2,256,8,160]{1,3,2,0:T(8,128)(2,1)}), bf16[2,256,8,160]{1,3,2,0:T(8,128)(2,1)}) %all-reduce.5.cloned.1.call-update) | async-done | bytes 1310736 | tf_op jit(solution)/shard_map/psum | solution.py:109
  308.7 35.2 %collective-permute-done.17 = bf16[640,1280]{1,0:T(8,128)(2,1)} collective-permute-done((bf16[640,1280]{1,0:T(8,128)(2,1)}, bf16[640,1280]{1,0:T(8,128)(2,1)}, u32[]{:S(2)}, u32[]{:S(2)}) %collective-permute-start.17) | collective-permute-done | bytes 1638432 | tf_op jit(solution)/shard_map/ppermute | solution.py:16
  344.0 5.0 fusion.80
  349.4 29.5 %collective-permute-done.23 = bf16[640,1280]{1,0:T(8,128)(2,1)} collective-permute-done((bf16[640,1280]{1,0:T(8,128)(2,1)}, bf16[640,1280]{1,0:T(8,128)(2,1)}, u32[]{:S(2)}, u32[]{:S(2)}) %collective-permute-start.23) | collective-permute-done | bytes 1638432 | tf_op jit(solution)/shard_map/ppermute | solution.py:16
  378.9 11.3 %multiply_convert_fusion.1 = (bf16[512,1280]{1,0:T(8,128)(2,1)}, f32[512,1280]{1,0:T(8,128)S(1)}, f32[512,1280]{1,0:T(8,128)S(1)}) fusion(bf16[640,1280]{1,0:T(8,128)(2,1)} %collective-permute-done.23, bf16[640,1280]{1,0:T(8,128)(2,1)} %maximum_select_fusion.5, pred[]{:T(512)S(6)} %eq.4, f32[512,1280]{1,0:T(8,128)S(1)} %get-tuple-element.47, ...), kind=kOutput, calls=%fused_computation.27 | convolution fusion | flops 1738342400 | bytes 12466177 | tf_op jit(solution)/shard_map/dot_general | solution.py:36
  390.2 22.1 %collective-permute-done.25 = bf16[640,1280]{1,0:T(8,128)(2,1)} collective-permute-done((bf16[640,1280]{1,0:T(8,128)(2,1)}, bf16[640,1280]{1,0:T(8,128)(2,1)}, u32[]{:S(2)}, u32[]{:S(2)}) %collective-permute-start.25) | collective-permute-done | bytes 1638432 | tf_op jit(solution)/shard_map/ppermute | solution.py:16
  412.3 5.8 add_convert_fusion
  418.1 6.5 multiply_reduce_fusion
  427.4 6.2 convolution_convert_fusion.5
  436.1 4.0 reshape.583
  462.9 6.5 reduce-scatter.9.cloned.1.call-done
  469.5 42.1 %reduce-scatter.11.cloned.1.call-done = bf16[192,1280]{1,0:T(8,128)(2,1)} async-done(((bf16[768,1280]{1,0:T(8,128)(2,1)}), bf16[192,1280]{1,0:T(8,128)(2,1)}) %reduce-scatter.11.cloned.1.call-update) | async-done | bytes 491536 | tf_op jit(solution)/shard_map/reduce_scatter | solution.py:52
  511.6 5.6 convolution_convert_fusion.1
  518.5 5.3 convolution_convert_fusion.2
  525.2 5.0 convolution_convert_fusion
  530.8 17.4 %psum.55 = f32[2560]{0:T(1024)S(1)} all-reduce(f32[2560]{0:T(1024)S(1)} %pad_maximum_fusion), channel_id=1, replica_groups=mesh['ctx'=8,'wshard'=4] {'wshard'}, use_global_device_ids=true, to_apply=%region_33.34 | all-reduce | flops 2560 | bytes 20480 | tf_op jit(solution)/shard_map/psum | solution.py:162
  554.1 37.8 %psum.52 = f32[1536]{0:T(1024)S(1)} all-reduce(f32[1536]{0:T(1024)S(1)} %pad_maximum_fusion.1), channel_id=1, replica_groups=mesh['ctx'=8,'wshard'=4] {'ctx','wshard'}, use_global_device_ids=true, to_apply=%region_25.26 | all-reduce | flops 1536 | bytes 12288 | tf_op jit(solution)/shard_map/psum | solution.py:160
  595.6 6.1 fusion.2
  601.7 37.5 %all-reduce.7.cloned.1.call-done = bf16[256,256]{0,1:T(8,128)(2,1)} async-done(((bf16[256,256]{0,1:T(8,128)(2,1)}), bf16[256,256]{0,1:T(8,128)(2,1)}) %all-reduce.7.cloned.1.call-update) | async-done | bytes 131088 | tf_op jit(solution)/shard_map/psum | solution.py:147
  644.9 18.2 %reduce-scatter.7.cloned.1.call-done = bf16[64,1280]{1,0:T(8,128)(2,1)} async-done(((bf16[256,1280]{1,0:T(8,128)(2,1)}), bf16[64,1280]{1,0:T(8,128)(2,1)}) %reduce-scatter.7.cloned.1.call-update) | async-done | bytes 163856 | tf_op jit(solution)/shard_map/reduce_scatter | solution.py:52
  664.9 55.3 %all-reduce.9.cloned.1.call-done = (bf16[192,256]{1,0:T(8,128)(2,1)}, bf16[192,1280]{1,0:T(8,128)(2,1)}) async-done(((bf16[192,256]{1,0:T(8,128)(2,1)}, bf16[192,1280]{1,0:T(8,128)(2,1)}), (bf16[192,256]{1,0:T(8,128)(2,1)}, bf16[192,1280]{1,0:T(8,128)(2,1)})) %all-reduce.9.cloned.1.call-update) | async-done | bytes 589840 | tf_op jit(solution)/shard_map/psum | solution.py:158
  723.8 60.4 %reduce-scatter.15.cloned.1.call-done = bf16[320,1280]{1,0:T(8,128)(2,1)} async-done(((bf16[1280,1280]{1,0:T(8,128)(2,1)}), bf16[320,1280]{1,0:T(8,128)(2,1)}) %reduce-scatter.15.cloned.1.call-update) | async-done | bytes 819216 | tf_op jit(solution)/shard_map/reduce_scatter | solution.py:52
  786.6 62.5 %reduce-scatter.13.cloned.1.call-done = bf16[320,1280]{1,0:T(8,128)(2,1)} async-done(((bf16[1280,1280]{1,0:T(8,128)(2,1)}), bf16[320,1280]{1,0:T(8,128)(2,1)}) %reduce-scatter.13.cloned.1.call-update) | async-done | bytes 819216 | tf_op jit(solution)/shard_map/reduce_scatter | solution.py:52
  851.5 62.4 %reduce-scatter.17.cloned.1.call-done = bf16[320,1280]{1,0:T(8,128)(2,1)} async-done(((bf16[1280,1280]{1,0:T(8,128)(2,1)}), bf16[320,1280]{1,0:T(8,128)(2,1)}) %reduce-scatter.17.cloned.1.call-update) | async-done | bytes 819216 | tf_op jit(solution)/shard_map/reduce_scatter | solution.py:52
  (302 shorter events, 165.1 us)
Async XLA Ops:
  7.2 298.2 %all-reduce.5.cloned.1.call-start = ((), (), s32[]{:S(2)}) async-start(), calls=%async_computation.6 | async-start | bytes 2621440 | tf_op jit(solution)/shard_map/psum | solution.py:109
  7.3 63.5 %collective-permute-start = (bf16[64,1280]{1,0:T(8,128)(2,1)}, bf16[64,1280]{1,0:T(8,128)(2,1)S(1)}, u32[]{:S(2)}, u32[]{:S(2)}) collective-permute-start(bf16[64,1280]{1,0:T(8,128)(2,1)} %param.18), channel_id=1, source_target_pairs={{0,1},{1,0},{2,3},{3,2},{4,5},{5,4},{6,7},{7,6},{8,9},{9,8},{10,11... | collective-permute-start | bytes 491528 | tf_op jit(solution)/shard_map/ppermute | solution.py:16
  10.3 14.3 %collective-permute-start.10 = (bf16[320]{0:T(512)(128)(2,1)}, bf16[320]{0:T(512)(128)(2,1)S(1)}, u32[]{:S(2)}, u32[]{:S(2)}) collective-permute-start(bf16[320]{0:T(512)(128)(2,1)} %param.19), channel_id=1, source_target_pairs={{0,1},{1,0},{2,3},{3,2},{4,5},{5,4},{6,7},{7,6},{8,9},{9,8},{10,11... | collective-permute-start | bytes 1928 | tf_op jit(solution)/shard_map/ppermute | solution.py:16
  10.4 15.7 %collective-permute-start.12 = (bf16[320]{0:T(512)(128)(2,1)}, bf16[320]{0:T(512)(128)(2,1)S(1)}, u32[]{:S(2)}, u32[]{:S(2)}) collective-permute-start(bf16[320]{0:T(512)(128)(2,1)} %param.20), channel_id=1, source_target_pairs={{0,1},{1,0},{2,3},{3,2},{4,5},{5,4},{6,7},{7,6},{8,9},{9,8},{10,11... | collective-permute-start | bytes 1928 | tf_op jit(solution)/shard_map/ppermute | solution.py:16
  12.4 60.1 %collective-permute-start.14 = (bf16[320,256]{1,0:T(8,128)(2,1)}, bf16[320,256]{1,0:T(8,128)(2,1)}, u32[]{:S(2)}, u32[]{:S(2)}) collective-permute-start(bf16[320,256]{1,0:T(8,128)(2,1)} %param.23), channel_id=1, source_target_pairs={{0,1},{1,0},{2,3},{3,2},{4,5},{5,4},{6,7},{7,6},{8,9},{9,8},{10,11... | collective-permute-start | bytes 491528 | tf_op jit(solution)/shard_map/ppermute | solution.py:16
  12.5 6.2 collective-permute-start.2
  22.4 46.6 %collective-permute-start.8 = (bf16[192,256]{1,0:T(8,128)(2,1)}, bf16[192,256]{1,0:T(8,128)(2,1)S(1)}, u32[]{:S(2)}, u32[]{:S(2)}) collective-permute-start(bf16[192,256]{1,0:T(8,128)(2,1)} %param.24), channel_id=1, source_target_pairs={{0,1},{1,0},{2,3},{3,2},{4,5},{5,4},{6,7},{7,6},{8,9},{9,8},{10,11... | collective-permute-start | bytes 294920 | tf_op jit(solution)/shard_map/ppermute | solution.py:16
  24.7 131.4 %collective-permute-start.6 = (bf16[192,1280]{1,0:T(8,128)(2,1)}, bf16[192,1280]{1,0:T(8,128)(2,1)}, u32[]{:S(2)}, u32[]{:S(2)}) collective-permute-start(bf16[192,1280]{1,0:T(8,128)(2,1)} %param.25), channel_id=1, source_target_pairs={{0,1},{1,0},{2,3},{3,2},{4,5},{5,4},{6,7},{7,6},{8,9},{9,8},{10,11... | collective-permute-start | bytes 1474568 | tf_op jit(solution)/shard_map/ppermute | solution.py:16
  26.1 10.6 %collective-permute-start.18 = (bf16[320]{0:T(512)(128)(2,1)}, bf16[320]{0:T(512)(128)(2,1)S(1)}, u32[]{:S(2)}, u32[]{:S(2)}) collective-permute-start(bf16[320]{0:T(512)(128)(2,1)} %param.27), channel_id=1, source_target_pairs={{0,1},{1,0},{2,3},{3,2},{4,5},{5,4},{6,7},{7,6},{8,9},{9,8},{10,11... | collective-permute-start | bytes 1928 | tf_op jit(solution)/shard_map/ppermute | solution.py:16
  44.9 4.5 collective-permute-start.5
  49.4 5.4 collective-permute-start.11
  54.8 4.5 collective-permute-start.13
  59.3 4.6 collective-permute-start.19
  63.9 4.6 collective-permute-start.21
  68.5 124.7 %collective-permute-start.16 = (bf16[320,1280]{1,0:T(8,128)(2,1)S(1)}, bf16[320,1280]{1,0:T(8,128)(2,1)}, u32[]{:S(2)}, u32[]{:S(2)}) collective-permute-start(bf16[320,1280]{1,0:T(8,128)(2,1)S(1)} %copy-done.20), channel_id=1, source_target_pairs={{0,1},{1,0},{2,3},{3,2},{4,5},{5,4},{6,7},{7,6},{8,9},{9,8},{10,11... | collective-permute-start | bytes 2457608 | tf_op jit(solution)/shard_map/ppermute | solution.py:16
  69.0 179.9 %collective-permute-start.22 = (bf16[320,1280]{1,0:T(8,128)(2,1)}, bf16[320,1280]{1,0:T(8,128)(2,1)}, u32[]{:S(2)}, u32[]{:S(2)}) collective-permute-start(bf16[320,1280]{1,0:T(8,128)(2,1)} %param.29), channel_id=1, source_target_pairs={{0,1},{1,0},{2,3},{3,2},{4,5},{5,4},{6,7},{7,6},{8,9},{9,8},{10,11... | collective-permute-start | bytes 2457608 | tf_op jit(solution)/shard_map/ppermute | solution.py:16
  70.8 38.7 %collective-permute-start.9 = (bf16[384,256]{1,0:T(8,128)(2,1)S(1)}, bf16[384,256]{1,0:T(8,128)(2,1)S(1)}, u32[]{:S(2)}, u32[]{:S(2)}) collective-permute-start(bf16[384,256]{1,0:T(8,128)(2,1)S(1)} %maximum_select_fusion.21), channel_id=1, source_target_pairs={{0,2},{1,3},{2,0},{3,1},{4,6},{5,7},{6,4},{7,5},{8,10},{9,11},{10,... | collective-permute-start | bytes 589832 | tf_op jit(solution)/shard_map/ppermute | solution.py:16
  72.5 44.0 %collective-permute-start.1 = (bf16[128,1280]{1,0:T(8,128)(2,1)S(1)}, bf16[128,1280]{1,0:T(8,128)(2,1)S(1)}, u32[]{:S(2)}, u32[]{:S(2)}) collective-permute-start(bf16[128,1280]{1,0:T(8,128)(2,1)S(1)} %maximum_select_fusion.19), channel_id=1, source_target_pairs={{0,2},{1,3},{2,0},{3,1},{4,6},{5,7},{6,4},{7,5},{8,10},{9,11},{10,... | collective-permute-start | bytes 983048 | tf_op jit(solution)/shard_map/ppermute | solution.py:16
  109.5 143.1 %collective-permute-start.24 = (bf16[320,1280]{1,0:T(8,128)(2,1)}, bf16[320,1280]{1,0:T(8,128)(2,1)}, u32[]{:S(2)}, u32[]{:S(2)}) collective-permute-start(bf16[320,1280]{1,0:T(8,128)(2,1)} %param.30), channel_id=1, source_target_pairs={{0,1},{1,0},{2,3},{3,2},{4,5},{5,4},{6,7},{7,6},{8,9},{9,8},{10,11... | collective-permute-start | bytes 2457608 | tf_op jit(solution)/shard_map/ppermute | solution.py:16
  116.5 13.7 %collective-permute-start.15 = (bf16[640,256]{1,0:T(8,128)(2,1)S(1)}, bf16[640,256]{1,0:T(8,128)(2,1)S(1)}, u32[]{:S(2)}, u32[]{:S(2)}) collective-permute-start(bf16[640,256]{1,0:T(8,128)(2,1)S(1)} %maximum_select_fusion.20), channel_id=1, source_target_pairs={{0,2},{1,3},{2,0},{3,1},{4,6},{5,7},{6,4},{7,5},{8,10},{9,11},{10,... | collective-permute-start | bytes 983048 | tf_op jit(solution)/shard_map/ppermute | solution.py:16
  157.8 80.7 %collective-permute-start.7 = (bf16[384,1280]{1,0:T(8,128)(2,1)S(1)}, bf16[384,1280]{1,0:T(8,128)(2,1)}, u32[]{:S(2)}, u32[]{:S(2)}) collective-permute-start(bf16[384,1280]{1,0:T(8,128)(2,1)S(1)} %maximum_select_fusion.7), channel_id=1, source_target_pairs={{0,2},{1,3},{2,0},{3,1},{4,6},{5,7},{6,4},{7,5},{8,10},{9,11},{10,... | collective-permute-start | bytes 2949128 | tf_op jit(solution)/shard_map/ppermute | solution.py:16
  196.3 147.5 %collective-permute-start.17 = (bf16[640,1280]{1,0:T(8,128)(2,1)}, bf16[640,1280]{1,0:T(8,128)(2,1)}, u32[]{:S(2)}, u32[]{:S(2)}) collective-permute-start(bf16[640,1280]{1,0:T(8,128)(2,1)} %maximum_select_fusion.4), channel_id=1, source_target_pairs={{0,2},{1,3},{2,0},{3,1},{4,6},{5,7},{6,4},{7,5},{8,10},{9,11},{10,... | collective-permute-start | bytes 4915208 | tf_op jit(solution)/shard_map/ppermute | solution.py:16
  248.8 220.7 %reduce-scatter.9.cloned.1.call-start = ((), (), s32[]{:S(2)}) async-start(), calls=%async_computation.9 | async-start | bytes 491520 | tf_op jit(solution)/shard_map/reduce_scatter | solution.py:52
  252.5 126.4 %collective-permute-start.23 = (bf16[640,1280]{1,0:T(8,128)(2,1)}, bf16[640,1280]{1,0:T(8,128)(2,1)}, u32[]{:S(2)}, u32[]{:S(2)}) collective-permute-start(bf16[640,1280]{1,0:T(8,128)(2,1)} %maximum_select_fusion.5), channel_id=1, source_target_pairs={{0,2},{1,3},{2,0},{3,1},{4,6},{5,7},{6,4},{7,5},{8,10},{9,11},{10,... | collective-permute-start | bytes 4915208 | tf_op jit(solution)/shard_map/ppermute | solution.py:16
  256.0 156.3 %collective-permute-start.25 = (bf16[640,1280]{1,0:T(8,128)(2,1)}, bf16[640,1280]{1,0:T(8,128)(2,1)}, u32[]{:S(2)}, u32[]{:S(2)}) collective-permute-start(bf16[640,1280]{1,0:T(8,128)(2,1)} %maximum_select_fusion.6), channel_id=1, source_target_pairs={{0,2},{1,3},{2,0},{3,1},{4,6},{5,7},{6,4},{7,5},{8,10},{9,11},{10,... | collective-permute-start | bytes 4915208 | tf_op jit(solution)/shard_map/ppermute | solution.py:16
  449.0 62.5 %reduce-scatter.11.cloned.1.call-start = ((), (), s32[]{:S(2)}) async-start(), calls=%async_computation.10 | async-start | bytes 2457600 | tf_op jit(solution)/shard_map/reduce_scatter | solution.py:52
  457.6 181.6 %all-reduce.7.cloned.1.call-start = ((), (), s32[]{:S(2)}) async-start(), calls=%async_computation.8 | async-start | bytes 262144 | tf_op jit(solution)/shard_map/psum | solution.py:147
  459.7 203.4 %reduce-scatter.7.cloned.1.call-start = ((), (), s32[]{:S(2)}) async-start(), calls=%async_computation.7 | async-start | bytes 819200 | tf_op jit(solution)/shard_map/reduce_scatter | solution.py:52
  462.9 257.3 %all-reduce.9.cloned.1.call-start = ((), (), s32[]{:S(2)}) async-start(), calls=%async_computation.14 | async-start | bytes 1179648 | tf_op jit(solution)/shard_map/psum | solution.py:158
  511.6 272.7 %reduce-scatter.15.cloned.1.call-start = ((), (), s32[]{:S(2)}) async-start(), calls=%async_computation.12 | async-start | bytes 4096000 | tf_op jit(solution)/shard_map/reduce_scatter | solution.py:52
  517.2 331.9 %reduce-scatter.13.cloned.1.call-start = ((), (), s32[]{:S(2)}) async-start(), calls=%async_computation.11 | async-start | bytes 4096000 | tf_op jit(solution)/shard_map/reduce_scatter | solution.py:52
  523.9 390.1 %reduce-scatter.17.cloned.1.call-start = ((), (), s32[]{:S(2)}) async-start(), calls=%async_computation.13 | async-start | bytes 4096000 | tf_op jit(solution)/shard_map/reduce_scatter | solution.py:52
  (73 other events, 2750.2 us)
Sparse Core Ops, SparseCore 0:
  248.9 56.4 all-reduce.4
  449.1 20.2 reduce-scatter.8
  471.8 39.7 reduce-scatter.10
  517.5 121.6 all-reduce.6
  641.9 21.1 reduce-scatter.6
  666.2 53.9 all-reduce.8
  722.6 61.5 reduce-scatter.14
  786.6 62.4 reduce-scatter.12
  851.5 62.3 reduce-scatter.16
